TPU v7x, 32 devices: a whole 2x2x4 slice. The times are simulated.
32 devices in a mesh: ctx: 16 (over z, y, x), tp: 2 (over core).
Axes of the slice: x: 2, y: 2, z: 4, core: 2. Of those that a mesh axis runs over, the one named last changes fastest.
Arguments:
- queries: bfloat16 [2048, 4096], P('ctx', 'tp'), may hold values from -220 to 220
- keys: bfloat16 [2048, 1024], P('ctx', 'tp'), may hold values from -6 to 6
- values: bfloat16 [2048, 1024], P('ctx', 'tp'), may hold values from -6 to 6
- out_weight: bfloat16 [4096, 4096], P('tp'), may hold values from -0.09375 to 0.09375
- residual: bfloat16 [2048, 4096], P('ctx', 'tp'), may hold values from -1.5 to 1.5
- norm_gain: bfloat16 [4096], P('tp'), may hold values from 0.5 to 1.5
- span_order: int32 [32], replicated, may hold values from 0 to 31, as said below
Outputs:
- normed: bfloat16 [2048, 4096], P('ctx', 'tp')
Inputs may be any that keep to these rules, and one draw needn't show every extreme that they name: `span_order`: every span appears in exactly one slot. The two slots of one index d of ctx (slots 2d and 2d + 1) hold a span p and its mirror, the span at the same place counted from the end of the sequence; which index holds which pair, and the order of the two, are drawn.
All inputs are finite; a program needn't handle non-finite values.
Results may differ from a plain program's by a relative error of at most 0.009.
Values may be sent and summed in bfloat16 or wider, within the bound.
A program may use at most 64 MiB of HBM per device.

v0:
```python
import math
import jax
import jax.numpy as jnp
from jax import lax
from jax.sharding import PartitionSpec as P

D = 4096
HEAD_SIZE = 128
EPSILON = 1e-05


def per_device(queries, keys, values, out_weight, residual, norm_gain, span_order):
    local_rows = queries.shape[0]
    span_rows = local_rows // 2
    heads = queries.shape[1] // HEAD_SIZE
    kv_heads = keys.shape[1] // HEAD_SIZE
    group_size = heads // kv_heads
    scale = 1.0 / math.sqrt(HEAD_SIZE)
    device = lax.axis_index("ctx")
    owned = lax.dynamic_slice_in_dim(span_order, 2 * device, 2)
    offsets = jnp.arange(span_rows, dtype=jnp.int32)
    query_pos = (owned[:, None] * span_rows + offsets[None, :]).reshape(local_rows)
    query_mat = queries.reshape(local_rows, kv_heads, group_size, HEAD_SIZE)
    fresh = (
        jnp.full((kv_heads, group_size, local_rows), -1e30, jnp.float32),
        jnp.zeros((kv_heads, group_size, local_rows), jnp.float32),
        jnp.zeros((kv_heads, group_size, local_rows, HEAD_SIZE), jnp.float32),
    )
    carry = fresh
    key_piece = lax.all_gather(keys, "ctx", axis=0, tiled=True)
    value_piece = lax.all_gather(values, "ctx", axis=0, tiled=True)
    count = key_piece.shape[0]
    spans = count // span_rows
    per_step = max(1, min(spans, 1024 // span_rows))
    while spans % per_step != 0:
        per_step = per_step - 1
    steps = spans // per_step
    block_rows = per_step * span_rows
    key_pos_all = (span_order[:, None] * span_rows + offsets[None, :]).reshape(steps, block_rows)
    key_blocks = key_piece.reshape(steps, block_rows, kv_heads, HEAD_SIZE)
    value_blocks = value_piece.reshape(steps, block_rows, kv_heads, HEAD_SIZE)

    def scan_step(state, item):
        running, total, accum = state
        key_pos, key_mat, value_mat = item
        scores = (
            jnp.einsum("qhgd,khd->hgqk", query_mat, key_mat, preferred_element_type=jnp.float32)
            * scale
        )
        allowed = (key_pos[None, :] <= query_pos[:, None])[None, None, :, :]
        scores = jnp.where(allowed, scores, -1e30)
        newmax = jnp.maximum(running, jnp.max(scores, axis=-1))
        weights = jnp.where(allowed, jnp.exp(scores - newmax[..., None]), 0.0)
        fade = jnp.exp(running - newmax)
        total = total * fade + jnp.sum(weights, axis=-1)
        accum = accum * fade[..., None] + jnp.einsum(
            "hgqk,khd->hgqd",
            weights.astype(jnp.bfloat16),
            value_mat,
            preferred_element_type=jnp.float32,
        )
        return ((newmax, total, accum), None)

    carry, unused = lax.scan(scan_step, carry, (key_pos_all, key_blocks, value_blocks))
    running, total, accum = carry
    attended = accum / total[..., None]
    attended = (
        jnp.transpose(attended, (2, 0, 1, 3))
        .reshape(local_rows, heads * HEAD_SIZE)
        .astype(jnp.bfloat16)
    )
    partial_value = jnp.dot(attended, out_weight, preferred_element_type=jnp.float32)
    share = lax.psum_scatter(
        partial_value.astype(jnp.bfloat16), "tp", scatter_dimension=1, tiled=True
    ).astype(jnp.float32)
    hidden = (residual.astype(jnp.float32) + share).astype(jnp.bfloat16)
    hidden_f = hidden.astype(jnp.float32)
    squares = lax.psum(jnp.sum(hidden_f * hidden_f, axis=1), "tp")
    factor = lax.rsqrt(squares / D + EPSILON)
    normed = hidden_f * factor[:, None] * norm_gain.astype(jnp.float32)[None, :]
    return normed.astype(jnp.bfloat16)


def solution(mesh):
    return jax.shard_map(
        per_device,
        mesh=mesh,
        in_specs=(
            P("ctx", "tp"),
            P("ctx", "tp"),
            P("ctx", "tp"),
            P("tp", None),
            P("ctx", "tp"),
            P("tp"),
            P(),
        ),
        out_specs=P("ctx", "tp"),
        check_vma=False,
    )
```

profile of v0, /device:TPU:0, one launch (start us, length us, event | category | flops | bytes accessed | tf_op | source)
XLA Modules:
  0.0 206.1 jit_solution(13089571367657228611)
XLA Ops:
  6.5 0.0 all-gather.3.cloned.1.call-start
  6.5 0.7 all-gather.3.cloned.1.call-update
  7.3 0.0 all-gather.5.cloned.1.call-start
  7.3 0.7 all-gather.5.cloned.1.call-update
  8.0 0.0 reduce-scatter.2.cloned.1.call-start
  8.1 1.3 copy.10
  9.4 1.0 copy.12
  10.4 0.7 broadcast_multiply_fusion
  11.1 0.1 add.60
  11.2 0.1 add.61
  11.2 0.1 add.62
  11.3 0.1 add.64
  11.4 0.7 dynamic-slice_multiply_fusion
  12.1 61.1 %all-gather.3.cloned.1.call-done = bf16[2048,512]{1,0:T(8,128)(2,1)} async-done(((bf16[128,512]{1,0:T(8,128)(2,1)}), bf16[2048,512]{1,0:T(8,128)(2,1)}) %all-gather.3.cloned.1.call-update) | async-done | bytes 2097168 | tf_op jit(solution)/shard_map/all_gather | solution.py:30
  73.2 2.5 %reshape.56 = bf16[2,1024,4,128]{3,2,1,0:T(4,128)(2,1)S(1)} reshape(bf16[2048,512]{1,0:T(8,128)(2,1)} %all-gather.3.cloned.1.call-done) | data formatting | bytes 4194304 | tf_op jit(solution)/shard_map/reshape | solution.py:40
  75.8 59.4 %all-gather.5.cloned.1.call-done = bf16[2048,512]{1,0:T(8,128)(2,1)} async-done(((bf16[128,512]{1,0:T(8,128)(2,1)}), bf16[2048,512]{1,0:T(8,128)(2,1)}) %all-gather.5.cloned.1.call-update) | async-done | bytes 2097168 | tf_op jit(solution)/shard_map/all_gather | solution.py:31
  135.2 4.0 %reshape.58 = bf16[2,1024,4,128]{3,2,1,0:T(4,128)(2,1)} reshape(bf16[2048,512]{1,0:T(8,128)(2,1)} %all-gather.5.cloned.1.call-done) | data formatting | bytes 4194304 | tf_op jit(solution)/shard_map/reshape | solution.py:41
  139.2 36.3 %while.15 = (s32[]{:T(128)}, f32[4,4,128]{2,1,0:T(4,128)S(1)}, f32[4,4,128]{2,1,0:T(4,128)S(1)}, f32[4,4,128,128]{3,2,1,0:T(8,128)}, s32[2,1024]{1,0:T(2,128)S(1...) while((s32[]{:T(128)}, f32[4,4,128]{2,1,0:T(4,128)S(1)}, ...), condition=%wide.region_3.4_spmd.clone, body=%wide.region_0.3_spmd.clone.sunk | while | flops 1101932672 | bytes 68303016 | solution.py:64
  139.2 0.1 iota_add_fusion.2
  139.3 0.1 le.33
  139.4 0.2 broadcast_compare_fusion.2
  139.6 2.0 constant_dynamic-slice_fusion.6
  141.6 5.6 %fusion.30 = (f32[4,4,128]{2,1,0:T(4,128)S(1)}, f32[4,1024,128,4]{2,1,3,0:T(8,128)}) fusion(pred[128,1024]{0,1:T(8,128)(4,1)S(1)} %broadcast_compare_fusion.2, bf16[128,4,4,128]{3,0,2,1:T(8,128)(2,1)} %get-tuple-element.216, bf16[1,1024,4,128]{3,2,1,0:T(4,128)(2,1)S(1)} %get-tuple-element.182), kind=kOutput, calls=%fused_computation.3.clone.1 | convolution fusion | flops 543160320 | bytes 10100736 | tf_op jit(solution)/shard_map/while/body/eval_jaxpr/qhgd,khd->hgqk/dot_general | solution.py:47
  147.2 0.0 copy-start
  147.2 4.6 %fusion.31 = f32[4,4,128]{2,1,0:T(4,128)S(1)} fusion(f32[4,1024,128,4]{2,1,3,0:T(8,128)} %get-tuple-element.184, f32[4,4,128]{2,1,0:T(4,128)S(1)} %select_maximum_fusion.2, pred[128,1024]{0,1:T(8,128)(4,1)S(1)} %broadcast_compare_fusion.2), kind=kLoop, calls=%fused_computation.5.clone.1 | loop fusion | flops 10483712 | bytes 8536064 | tf_op jit(solution)/shard_map/while/body/eval_jaxpr/reduce_sum | solution.py:55
  151.8 1.2 copy-done
  153.0 3.8 %fusion.33 = f32[4,4,128,128]{3,2,1,0:T(8,128)} fusion(f32[4,1024,128,4]{2,1,3,0:T(8,128)S(1)} %copy-done, f32[4,4,128]{2,1,0:T(4,128)S(1)} %select_maximum_fusion.2, pred[128,1024]{0,1:T(8,128)(4,1)S(1)} %broadcast_compare_fusion.2, bf16[1,1024,4,128]{3,2,1,0:T(4,128)(2,1)S(1)} %get-tuple-element.186, f32[4,4,128,128]{3,2,1,0:T(8,128)} %get-tuple-element.202, ...), kind=kOutput, calls=%fused_computation.8.clone.1 | convolution fusion | flops 548143104 | bytes 11681793 | tf_op jit(solution)/shard_map/while/body/eval_jaxpr/hgqk,khd->hgqd/dot_general | solution.py:56
  156.8 0.1 iota_add_fusion.2
  156.9 0.1 le.33
  157.0 0.2 broadcast_compare_fusion.2
  157.2 2.0 constant_dynamic-slice_fusion.6
  159.2 5.6 %fusion.30 = (f32[4,4,128]{2,1,0:T(4,128)S(1)}, f32[4,1024,128,4]{2,1,3,0:T(8,128)}) fusion(pred[128,1024]{0,1:T(8,128)(4,1)S(1)} %broadcast_compare_fusion.2, bf16[128,4,4,128]{3,0,2,1:T(8,128)(2,1)} %get-tuple-element.216, bf16[1,1024,4,128]{3,2,1,0:T(4,128)(2,1)S(1)} %get-tuple-element.182), kind=kOutput, calls=%fused_computation.3.clone.1 | convolution fusion | flops 543160320 | bytes 10100736 | tf_op jit(solution)/shard_map/while/body/eval_jaxpr/qhgd,khd->hgqk/dot_general | solution.py:47
  164.8 0.0 copy-start
  164.8 4.6 %fusion.31 = f32[4,4,128]{2,1,0:T(4,128)S(1)} fusion(f32[4,1024,128,4]{2,1,3,0:T(8,128)} %get-tuple-element.184, f32[4,4,128]{2,1,0:T(4,128)S(1)} %select_maximum_fusion.2, pred[128,1024]{0,1:T(8,128)(4,1)S(1)} %broadcast_compare_fusion.2), kind=kLoop, calls=%fused_computation.5.clone.1 | loop fusion | flops 10483712 | bytes 8536064 | tf_op jit(solution)/shard_map/while/body/eval_jaxpr/reduce_sum | solution.py:55
  169.5 1.2 copy-done
  170.6 4.8 %fusion.33 = f32[4,4,128,128]{3,2,1,0:T(8,128)} fusion(f32[4,1024,128,4]{2,1,3,0:T(8,128)S(1)} %copy-done, f32[4,4,128]{2,1,0:T(4,128)S(1)} %select_maximum_fusion.2, pred[128,1024]{0,1:T(8,128)(4,1)S(1)} %broadcast_compare_fusion.2, bf16[1,1024,4,128]{3,2,1,0:T(4,128)(2,1)S(1)} %get-tuple-element.186, f32[4,4,128,128]{3,2,1,0:T(8,128)} %get-tuple-element.202, ...), kind=kOutput, calls=%fused_computation.8.clone.1 | convolution fusion | flops 548143104 | bytes 11681793 | tf_op jit(solution)/shard_map/while/body/eval_jaxpr/hgqk,khd->hgqd/dot_general | solution.py:56
  175.5 1.6 copy.14
  177.0 0.1 divide_convert_fusion
  177.2 0.0 copy-start.2
  177.2 0.0 copy-start.1
  177.2 9.2 %convolution_convert_fusion = bf16[128,4096]{1,0:T(8,128)(2,1)} fusion(bf16[128,2048]{0,1:T(8,128)(2,1)S(1)} %bitcast.49, bf16[2048,4096]{1,0:T(8,128)(2,1)} %param.12), kind=kOutput, calls=%fused_computation.25 | convolution fusion | flops 2148007936 | bytes 18350080 | tf_op jit(solution)/shard_map/dot_general | solution.py:72
  186.4 0.0 reduce-scatter.2.cloned.1.call-update
  186.4 0.0 copy-done.2
  186.4 7.3 %reduce-scatter.2.cloned.1.call-done = bf16[128,2048]{1,0:T(8,128)(2,1)} async-done(((bf16[128,4096]{1,0:T(8,128)(2,1)}), bf16[128,2048]{1,0:T(8,128)(2,1)}) %reduce-scatter.2.cloned.1.call-update) | async-done | bytes 524304 | tf_op jit(solution)/shard_map/reduce_scatter | solution.py:73
  193.8 0.0 copy-done.1
  193.8 1.3 fusion.16
  195.1 2.5 %psum.7 = f32[128]{0:T(128)S(1)} all-reduce(f32[128]{0:T(128)S(1)} %fusion.16), channel_id=1, replica_groups=mesh['ctx'=16,'tp'=2] {'tp'}, use_global_device_ids=true, to_apply=%region_6.7 | all-reduce | flops 128 | bytes 1024 | tf_op jit(solution)/shard_map/psum | solution.py:78
  197.5 2.0 fusion.18
  (15 shorter events, 0.1 us)
Async XLA Ops:
  6.5 66.7 %all-gather.3.cloned.1.call-start = ((), (), s32[]{:S(2)}) async-start(), calls=%async_computation.1 | async-start | bytes 2228224 | tf_op jit(solution)/shard_map/all_gather | solution.py:30
  7.3 128.0 %all-gather.5.cloned.1.call-start = ((), (), s32[]{:S(2)}) async-start(), calls=%async_computation.2 | async-start | bytes 2228224 | tf_op jit(solution)/shard_map/all_gather | solution.py:31
  8.0 185.7 %reduce-scatter.2.cloned.1.call-start = ((), (), s32[]{:S(2)}) async-start(), calls=%async_computation.3 | async-start | bytes 1572864 | tf_op jit(solution)/shard_map/reduce_scatter | solution.py:73
  147.2 5.8 %copy-start = (f32[4,1024,128,4]{2,1,3,0:T(8,128)S(1)}, f32[4,1024,128,4]{2,1,3,0:T(8,128)}, u32[]{:S(2)}) copy-start(f32[4,1024,128,4]{2,1,3,0:T(8,128)} %get-tuple-element.184) | copy-start | bytes 25165828 | tf_op jit(solution)/shard_map/while
  164.8 5.8 %copy-start = (f32[4,1024,128,4]{2,1,3,0:T(8,128)S(1)}, f32[4,1024,128,4]{2,1,3,0:T(8,128)}, u32[]{:S(2)}) copy-start(f32[4,1024,128,4]{2,1,3,0:T(8,128)} %get-tuple-element.184) | copy-start | bytes 25165828 | tf_op jit(solution)/shard_map/while
  177.2 9.2 %copy-start.2 = (bf16[2048]{0:T(1024)(128)(2,1)S(1)}, bf16[2048]{0:T(1024)(128)(2,1)}, u32[]{:S(2)}) copy-start(bf16[2048]{0:T(1024)(128)(2,1)} %param.14) | copy-start | bytes 12292
  177.2 16.6 %copy-start.1 = (bf16[128,2048]{1,0:T(8,128)(2,1)S(1)}, bf16[128,2048]{1,0:T(8,128)(2,1)}, u32[]{:S(2)}) copy-start(bf16[128,2048]{1,0:T(8,128)(2,1)} %param.13) | copy-start | bytes 1572868
Sparse Core Ops, SparseCore 0:
  10.1 63.0 all-gather.2
  76.0 59.1 all-gather.4
  186.5 7.1 reduce-scatter.1
where the time goes:
time: 207 us; the launch traced here: 206 us
  waiting for transfers between devices  129 us (62%)
  matrix products  29.1 us (14%)
  local copies, waits for them, and re-layouts  17.2 us (8%)
  other arithmetic  14.7 us (7%)
  between operations  13.2 us (6%)
  blocking collectives  2.46 us (1%)
    all_gather x1, waiting for transfers between devices, per_device(): key_piece = lax.all_gather(keys, 'ctx', axis=0, tiled=True)  61.1 us
    all_gather x1, waiting for transfers between devices, per_device(): value_piece = lax.all_gather(values, 'ctx', axis=0, tiled=True)  59.4 us
    dot_general x2, matrix products, scan_step(): jnp.einsum('qhgd,khd->hgqk', query_mat, key_mat, preferred_element_type=j...  11.3 us
    reduce_sum x2, other arithmetic, scan_step(): total = total * fade + jnp.sum(weights, axis=-1)  9.21 us
    dot_general x1, matrix products, per_device(): jnp.dot(attended, out_weight, preferred_element_type=jnp.float32)  9.19 us
    dot_general x2, matrix products, scan_step(): jnp.einsum('hgqk,khd->hgqd', weights.astype(jnp.bfloat16), value_mat, pre...  8.61 us
    reduce_scatter x1, waiting for transfers between devices, per_device(): lax.psum_scatter(partial_value.astype(jnp.bfloat16), 'tp', scatter_dimens...  7.33 us
  transfers between devices with their start and end apart: 3, of which 3 were waited for; matrix products, arithmetic and copies ran while one was open for 3% of the time, Pallas kernels for 0%

commit v1 on v0

--- a/solution.py
+++ b/solution.py
@@ -28,7 +28,12 @@
     )
     carry = fresh
     key_piece = lax.all_gather(keys, "ctx", axis=0, tiled=True)
-    value_piece = lax.all_gather(values, "ctx", axis=0, tiled=True)
+    ring = [values]
+    for hop in range(15):
+        ring.append(lax.ppermute(ring[-1], "ctx", [(dev, (dev + 1) % 16) for dev in range(16)]))
+    value_piece = jnp.roll(
+        jnp.concatenate(ring[::-1], axis=0), (lax.axis_index("ctx") + 1) * ring[0].shape[0], axis=0
+    )
     count = key_piece.shape[0]
     spans = count // span_rows
     per_step = max(1, min(spans, 1024 // span_rows))

time: 207 us -> 246 us (1.19)
  waiting for transfers between devices: 129 us -> 165 us
  starting transfers between devices: 0.08 us -> 3.05 us
    ppermute x0 -> x15, waiting for transfers between devices: none -> 127 us  [per_device(): lax.ppermute(ring[-1], 'ctx', [(dev, (dev + 1) % 16) for dev in range(16)])]
    all_gather x1 -> x0, waiting for transfers between devices: 59.4 us -> none  [per_device(): value_piece = lax.all_gather(values, 'ctx', axis=0, tiled=True)]
    all_gather x1, waiting for transfers between devices: 61.1 us -> 31.1 us  [per_device(): key_piece = lax.all_gather(keys, 'ctx', axis=0, tiled=True)]
    ppermute x0 -> x15, starting transfers between devices: none -> 3 us  [per_device(): lax.ppermute(ring[-1], 'ctx', [(dev, (dev + 1) % 16) for dev in range(16)])]
  transfers between devices with their start and end apart: 3 -> 17, of which waited for: 3 -> 17; matrix products, arithmetic and copies ran while one was open for 3% -> 3% of each run, Pallas kernels for 0% -> 0%
where the time goes in v1:
time: 246 us
  waiting for transfers between devices  165 us (67%)
  matrix products  27 us (11%)
  local copies, waits for them, and re-layouts  19.1 us (8%)
  other arithmetic  14.7 us (6%)
  between operations  13.8 us (6%)
  starting transfers between devices  3.05 us (1%)
  blocking collectives  2.46 us (1%)
    ppermute x15, waiting for transfers between devices, per_device(): lax.ppermute(ring[-1], 'ctx', [(dev, (dev + 1) % 16) for dev in range(16)])  127 us
    all_gather x1, waiting for transfers between devices, per_device(): key_piece = lax.all_gather(keys, 'ctx', axis=0, tiled=True)  31.1 us
    reduce_sum x2, other arithmetic, scan_step(): total = total * fade + jnp.sum(weights, axis=-1)  9.21 us
    dot_general x2, matrix products, scan_step(): jnp.einsum('qhgd,khd->hgqk', query_mat, key_mat, preferred_element_type=j...  9.21 us
    dot_general x1, matrix products, per_device(): jnp.dot(attended, out_weight, preferred_element_type=jnp.float32)  9.2 us
    dot_general x2, matrix products, scan_step(): jnp.einsum('hgqk,khd->hgqd', weights.astype(jnp.bfloat16), value_mat, pre...  8.61 us
    reduce_scatter x1, waiting for transfers between devices, per_device(): lax.psum_scatter(partial_value.astype(jnp.bfloat16), 'tp', scatter_dimens...  7.33 us
  transfers between devices with their start and end apart: 17, of which 17 were waited for; matrix products, arithmetic and copies ran while one was open for 3% of the time, Pallas kernels for 0%

profile of v1, /device:TPU:0, one launch (start us, length us, event | category | flops | bytes accessed | tf_op | source)
XLA Modules:
  0.0 245.6 jit_solution(11424971565221419289)
XLA Ops:
  6.5 3.0 %collective-permute-start = (bf16[128,512]{1,0:T(8,128)(2,1)}, bf16[128,512]{1,0:T(8,128)(2,1)S(1)}, u32[]{:S(2)}, u32[]{:S(2)}) collective-permute-start(bf16[128,512]{1,0:T(8,128)(2,1)} %param.11), channel_id=1, source_target_pairs={{0,2},{2,4},{4,6},{6,8},{8,10},{10,12},{12,14},{14,16},{16,18},{18... | collective-permute-start | bytes 393224 | tf_op jit(solution)/shard_map/ppermute | solution.py:33
  9.5 7.8 %collective-permute-done = bf16[128,512]{1,0:T(8,128)(2,1)S(1)} collective-permute-done((bf16[128,512]{1,0:T(8,128)(2,1)}, bf16[128,512]{1,0:T(8,128)(2,1)S(1)}, u32[]{:S(2)}, u32[]{:S(2)}) %collective-permute-start) | collective-permute-done | bytes 131104 | tf_op jit(solution)/shard_map/ppermute | solution.py:33
  17.3 8.6 %collective-permute-done.1 = bf16[128,512]{1,0:T(8,128)(2,1)S(1)} collective-permute-done((bf16[128,512]{1,0:T(8,128)(2,1)S(1)}, bf16[128,512]{1,0:T(8,128)(2,1)S(1)}, u32[]{:S(2)}, u32[]{:S(2)}) %collective-permute-start.1) | collective-permute-done | bytes 131104 | tf_op jit(solution)/shard_map/ppermute | solution.py:33
  25.8 8.6 %collective-permute-done.2 = bf16[128,512]{1,0:T(8,128)(2,1)S(1)} collective-permute-done((bf16[128,512]{1,0:T(8,128)(2,1)S(1)}, bf16[128,512]{1,0:T(8,128)(2,1)S(1)}, u32[]{:S(2)}, u32[]{:S(2)}) %collective-permute-start.2) | collective-permute-done | bytes 131104 | tf_op jit(solution)/shard_map/ppermute | solution.py:33
  34.4 8.6 %collective-permute-done.3 = bf16[128,512]{1,0:T(8,128)(2,1)S(1)} collective-permute-done((bf16[128,512]{1,0:T(8,128)(2,1)S(1)}, bf16[128,512]{1,0:T(8,128)(2,1)S(1)}, u32[]{:S(2)}, u32[]{:S(2)}) %collective-permute-start.3) | collective-permute-done | bytes 131104 | tf_op jit(solution)/shard_map/ppermute | solution.py:33
  43.0 8.6 %collective-permute-done.4 = bf16[128,512]{1,0:T(8,128)(2,1)S(1)} collective-permute-done((bf16[128,512]{1,0:T(8,128)(2,1)S(1)}, bf16[128,512]{1,0:T(8,128)(2,1)S(1)}, u32[]{:S(2)}, u32[]{:S(2)}) %collective-permute-start.4) | collective-permute-done | bytes 131104 | tf_op jit(solution)/shard_map/ppermute | solution.py:33
  51.5 8.9 %collective-permute-done.5 = bf16[128,512]{1,0:T(8,128)(2,1)S(1)} collective-permute-done((bf16[128,512]{1,0:T(8,128)(2,1)S(1)}, bf16[128,512]{1,0:T(8,128)(2,1)S(1)}, u32[]{:S(2)}, u32[]{:S(2)}) %collective-permute-start.5) | collective-permute-done | bytes 131104 | tf_op jit(solution)/shard_map/ppermute | solution.py:33
  60.4 9.9 %collective-permute-done.6 = bf16[128,512]{1,0:T(8,128)(2,1)S(1)} collective-permute-done((bf16[128,512]{1,0:T(8,128)(2,1)S(1)}, bf16[128,512]{1,0:T(8,128)(2,1)S(1)}, u32[]{:S(2)}, u32[]{:S(2)}) %collective-permute-start.6) | collective-permute-done | bytes 131104 | tf_op jit(solution)/shard_map/ppermute | solution.py:33
  70.3 9.1 %collective-permute-done.7 = bf16[128,512]{1,0:T(8,128)(2,1)S(1)} collective-permute-done((bf16[128,512]{1,0:T(8,128)(2,1)S(1)}, bf16[128,512]{1,0:T(8,128)(2,1)S(1)}, u32[]{:S(2)}, u32[]{:S(2)}) %collective-permute-start.7) | collective-permute-done | bytes 131104 | tf_op jit(solution)/shard_map/ppermute | solution.py:33
  79.4 8.6 %collective-permute-done.8 = bf16[128,512]{1,0:T(8,128)(2,1)S(1)} collective-permute-done((bf16[128,512]{1,0:T(8,128)(2,1)S(1)}, bf16[128,512]{1,0:T(8,128)(2,1)S(1)}, u32[]{:S(2)}, u32[]{:S(2)}) %collective-permute-start.8) | collective-permute-done | bytes 131104 | tf_op jit(solution)/shard_map/ppermute | solution.py:33
  88.0 8.6 %collective-permute-done.9 = bf16[128,512]{1,0:T(8,128)(2,1)S(1)} collective-permute-done((bf16[128,512]{1,0:T(8,128)(2,1)S(1)}, bf16[128,512]{1,0:T(8,128)(2,1)S(1)}, u32[]{:S(2)}, u32[]{:S(2)}) %collective-permute-start.9) | collective-permute-done | bytes 131104 | tf_op jit(solution)/shard_map/ppermute | solution.py:33
  96.5 8.6 %collective-permute-done.10 = bf16[128,512]{1,0:T(8,128)(2,1)S(1)} collective-permute-done((bf16[128,512]{1,0:T(8,128)(2,1)S(1)}, bf16[128,512]{1,0:T(8,128)(2,1)S(1)}, u32[]{:S(2)}, u32[]{:S(2)}) %collective-permute-start.10) | collective-permute-done | bytes 131104 | tf_op jit(solution)/shard_map/ppermute | solution.py:33
  105.1 8.6 %collective-permute-done.11 = bf16[128,512]{1,0:T(8,128)(2,1)S(1)} collective-permute-done((bf16[128,512]{1,0:T(8,128)(2,1)S(1)}, bf16[128,512]{1,0:T(8,128)(2,1)S(1)}, u32[]{:S(2)}, u32[]{:S(2)}) %collective-permute-start.11) | collective-permute-done | bytes 131104 | tf_op jit(solution)/shard_map/ppermute | solution.py:33
  113.7 8.8 %collective-permute-done.12 = bf16[128,512]{1,0:T(8,128)(2,1)S(1)} collective-permute-done((bf16[128,512]{1,0:T(8,128)(2,1)S(1)}, bf16[128,512]{1,0:T(8,128)(2,1)S(1)}, u32[]{:S(2)}, u32[]{:S(2)}) %collective-permute-start.12) | collective-permute-done | bytes 131104 | tf_op jit(solution)/shard_map/ppermute | solution.py:33
  122.6 0.7 broadcast_multiply_fusion
  123.2 0.1 add.73
  123.4 0.1 add.75
  123.5 8.6 %collective-permute-done.13 = bf16[128,512]{1,0:T(8,128)(2,1)S(1)} collective-permute-done((bf16[128,512]{1,0:T(8,128)(2,1)S(1)}, bf16[128,512]{1,0:T(8,128)(2,1)S(1)}, u32[]{:S(2)}, u32[]{:S(2)}) %collective-permute-start.13) | collective-permute-done | bytes 131104 | tf_op jit(solution)/shard_map/ppermute | solution.py:33
  132.2 1.3 copy.10
  133.6 1.0 copy.12
  134.6 0.7 dynamic-slice_multiply_fusion
  135.3 5.4 %collective-permute-done.14 = bf16[128,512]{1,0:T(8,128)(2,1)S(1)} collective-permute-done((bf16[128,512]{1,0:T(8,128)(2,1)S(1)}, bf16[128,512]{1,0:T(8,128)(2,1)S(1)}, u32[]{:S(2)}, u32[]{:S(2)}) %collective-permute-start.14) | collective-permute-done | bytes 131104 | tf_op jit(solution)/shard_map/ppermute | solution.py:33
  141.3 1.5 constant_dynamic-slice_fusion.3
  142.8 2.5 %reshape.58 = bf16[2,1024,4,128]{3,2,1,0:T(4,128)(2,1)S(1)} reshape(bf16[2048,512]{1,0:T(8,128)(2,1)} %constant_dynamic-slice_fusion.3) | data formatting | bytes 4194304 | tf_op jit(solution)/shard_map/reshape | solution.py:46
  145.4 31.1 %all-gather.2.cloned.1.call-done = bf16[2048,512]{1,0:T(8,128)(2,1)} async-done(((bf16[128,512]{1,0:T(8,128)(2,1)}), bf16[2048,512]{1,0:T(8,128)(2,1)}) %all-gather.2.cloned.1.call-update) | async-done | bytes 2097168 | tf_op jit(solution)/shard_map/all_gather | solution.py:30
  176.4 4.0 %reshape.56 = bf16[2,1024,4,128]{3,2,1,0:T(4,128)(2,1)} reshape(bf16[2048,512]{1,0:T(8,128)(2,1)} %all-gather.2.cloned.1.call-done) | data formatting | bytes 4194304 | tf_op jit(solution)/shard_map/reshape | solution.py:45
  180.4 34.2 %while.15 = (s32[]{:T(128)}, f32[4,4,128]{2,1,0:T(4,128)S(1)}, f32[4,4,128]{2,1,0:T(4,128)S(1)}, f32[4,4,128,128]{3,2,1,0:T(8,128)}, s32[2,1024]{1,0:T(2,128)S(1...) while((s32[]{:T(128)}, f32[4,4,128]{2,1,0:T(4,128)S(1)}, ...), condition=%wide.region_3.4_spmd.clone, body=%wide.region_0.3_spmd.clone.sunk | while | flops 1101932672 | bytes 70400192 | solution.py:69
  180.5 0.1 le.33
  180.6 0.2 broadcast_compare_fusion.2
  180.8 2.0 constant_dynamic-slice_fusion.7
  182.8 4.6 %fusion.30 = (f32[4,4,128]{2,1,0:T(4,128)S(1)}, f32[4,1024,128,4]{2,1,3,0:T(8,128)}) fusion(pred[128,1024]{0,1:T(8,128)(4,1)S(1)} %broadcast_compare_fusion.2, bf16[128,4,4,128]{3,0,2,1:T(8,128)(2,1)S(1)} %copy-done.1, bf16[1,1024,4,128]{3,2,1,0:T(4,128)(2,1)S(1)} %get-tuple-element.182), kind=kOutput, calls=%fused_computation.3.clone.1 | convolution fusion | flops 543160320 | bytes 10100736 | tf_op jit(solution)/shard_map/while/body/eval_jaxpr/qhgd,khd->hgqk/dot_general | solution.py:52
  187.4 4.6 %fusion.31 = f32[4,4,128]{2,1,0:T(4,128)S(1)} fusion(f32[4,1024,128,4]{2,1,3,0:T(8,128)} %get-tuple-element.184, f32[4,4,128]{2,1,0:T(4,128)S(1)} %select_maximum_fusion.2, pred[128,1024]{0,1:T(8,128)(4,1)S(1)} %broadcast_compare_fusion.2), kind=kLoop, calls=%fused_computation.5.clone.1 | loop fusion | flops 10483712 | bytes 8536064 | tf_op jit(solution)/shard_map/while/body/eval_jaxpr/reduce_sum | solution.py:60
  192.0 1.2 copy-done
  193.2 3.8 %fusion.33 = f32[4,4,128,128]{3,2,1,0:T(8,128)} fusion(f32[4,1024,128,4]{2,1,3,0:T(8,128)S(1)} %copy-done, f32[4,4,128]{2,1,0:T(4,128)S(1)} %select_maximum_fusion.2, pred[128,1024]{0,1:T(8,128)(4,1)S(1)} %broadcast_compare_fusion.2, bf16[1,1024,4,128]{3,2,1,0:T(4,128)(2,1)S(1)} %get-tuple-element.186, f32[4,4,128,128]{3,2,1,0:T(8,128)} %get-tuple-element.202, ...), kind=kOutput, calls=%fused_computation.8.clone.1 | convolution fusion | flops 548143104 | bytes 11681793 | tf_op jit(solution)/shard_map/while/body/eval_jaxpr/hgqk,khd->hgqd/dot_general | solution.py:61
  197.1 0.1 le.33
  197.2 0.2 broadcast_compare_fusion.2
  197.4 2.0 constant_dynamic-slice_fusion.7
  199.4 4.6 %fusion.30 = (f32[4,4,128]{2,1,0:T(4,128)S(1)}, f32[4,1024,128,4]{2,1,3,0:T(8,128)}) fusion(pred[128,1024]{0,1:T(8,128)(4,1)S(1)} %broadcast_compare_fusion.2, bf16[128,4,4,128]{3,0,2,1:T(8,128)(2,1)S(1)} %copy-done.1, bf16[1,1024,4,128]{3,2,1,0:T(4,128)(2,1)S(1)} %get-tuple-element.182), kind=kOutput, calls=%fused_computation.3.clone.1 | convolution fusion | flops 543160320 | bytes 10100736 | tf_op jit(solution)/shard_map/while/body/eval_jaxpr/qhgd,khd->hgqk/dot_general | solution.py:52
  204.0 4.6 %fusion.31 = f32[4,4,128]{2,1,0:T(4,128)S(1)} fusion(f32[4,1024,128,4]{2,1,3,0:T(8,128)} %get-tuple-element.184, f32[4,4,128]{2,1,0:T(4,128)S(1)} %select_maximum_fusion.2, pred[128,1024]{0,1:T(8,128)(4,1)S(1)} %broadcast_compare_fusion.2), kind=kLoop, calls=%fused_computation.5.clone.1 | loop fusion | flops 10483712 | bytes 8536064 | tf_op jit(solution)/shard_map/while/body/eval_jaxpr/reduce_sum | solution.py:60
  208.6 1.2 copy-done
  209.8 4.8 %fusion.33 = f32[4,4,128,128]{3,2,1,0:T(8,128)} fusion(f32[4,1024,128,4]{2,1,3,0:T(8,128)S(1)} %copy-done, f32[4,4,128]{2,1,0:T(4,128)S(1)} %select_maximum_fusion.2, pred[128,1024]{0,1:T(8,128)(4,1)S(1)} %broadcast_compare_fusion.2, bf16[1,1024,4,128]{3,2,1,0:T(4,128)(2,1)S(1)} %get-tuple-element.186, f32[4,4,128,128]{3,2,1,0:T(8,128)} %get-tuple-element.202, ...), kind=kOutput, calls=%fused_computation.8.clone.1 | convolution fusion | flops 548143104 | bytes 11681793 | tf_op jit(solution)/shard_map/while/body/eval_jaxpr/hgqk,khd->hgqd/dot_general | solution.py:61
  214.6 1.6 copy.14
  216.2 0.1 divide_convert_fusion
  216.4 9.2 %convolution_convert_fusion = bf16[128,4096]{1,0:T(8,128)(2,1)} fusion(bf16[128,2048]{0,1:T(8,128)(2,1)S(1)} %bitcast.49, bf16[2048,4096]{1,0:T(8,128)(2,1)} %param.12), kind=kOutput, calls=%fused_computation.25 | convolution fusion | flops 2148007936 | bytes 18350080 | tf_op jit(solution)/shard_map/dot_general | solution.py:77
  225.6 7.3 %reduce-scatter.2.cloned.1.call-done = bf16[128,2048]{1,0:T(8,128)(2,1)} async-done(((bf16[128,4096]{1,0:T(8,128)(2,1)}), bf16[128,2048]{1,0:T(8,128)(2,1)}) %reduce-scatter.2.cloned.1.call-update) | async-done | bytes 524304 | tf_op jit(solution)/shard_map/reduce_scatter | solution.py:78
  232.9 1.3 fusion.16
  234.2 2.5 %psum.7 = f32[128]{0:T(128)S(1)} all-reduce(f32[128]{0:T(128)S(1)} %fusion.16), channel_id=1, replica_groups=mesh['ctx'=16,'tp'=2] {'tp'}, use_global_device_ids=true, to_apply=%region_6.7 | all-reduce | flops 128 | bytes 1024 | tf_op jit(solution)/shard_map/psum | solution.py:83
  236.7 2.0 fusion.18
  (81 shorter events, 0.9 us)
Async XLA Ops:
  6.5 134.5 %copy-start.3 = (bf16[128,512]{1,0:T(8,128)(2,1)S(1)}, bf16[128,512]{1,0:T(8,128)(2,1)}, u32[]{:S(2)}) copy-start(bf16[128,512]{1,0:T(8,128)(2,1)} %param.11) | copy-start | bytes 393220
  6.5 169.9 %all-gather.2.cloned.1.call-start = ((), (), s32[]{:S(2)}) async-start(), calls=%async_computation.1 | async-start | bytes 2228224 | tf_op jit(solution)/shard_map/all_gather | solution.py:30
  6.5 10.7 %collective-permute-start = (bf16[128,512]{1,0:T(8,128)(2,1)}, bf16[128,512]{1,0:T(8,128)(2,1)S(1)}, u32[]{:S(2)}, u32[]{:S(2)}) collective-permute-start(bf16[128,512]{1,0:T(8,128)(2,1)} %param.11), channel_id=1, source_target_pairs={{0,2},{2,4},{4,6},{6,8},{8,10},{10,12},{12,14},{14,16},{16,18},{18... | collective-permute-start | bytes 393224 | tf_op jit(solution)/shard_map/ppermute | solution.py:33
  17.3 8.6 %collective-permute-start.1 = (bf16[128,512]{1,0:T(8,128)(2,1)S(1)}, bf16[128,512]{1,0:T(8,128)(2,1)S(1)}, u32[]{:S(2)}, u32[]{:S(2)}) collective-permute-start(bf16[128,512]{1,0:T(8,128)(2,1)S(1)} %collective-permute-done), channel_id=1, source_target_pairs={{0,2},{2,4},{4,6},{6,8},{8,10},{10,12},{12,14},{14,16},{16,18},{18... | collective-permute-start | bytes 393224 | tf_op jit(solution)/shard_map/ppermute | solution.py:33
  25.8 8.6 %collective-permute-start.2 = (bf16[128,512]{1,0:T(8,128)(2,1)S(1)}, bf16[128,512]{1,0:T(8,128)(2,1)S(1)}, u32[]{:S(2)}, u32[]{:S(2)}) collective-permute-start(bf16[128,512]{1,0:T(8,128)(2,1)S(1)} %collective-permute-done.1), channel_id=1, source_target_pairs={{0,2},{2,4},{4,6},{6,8},{8,10},{10,12},{12,14},{14,16},{16,18},{18... | collective-permute-start | bytes 393224 | tf_op jit(solution)/shard_map/ppermute | solution.py:33
  34.4 8.6 %collective-permute-start.3 = (bf16[128,512]{1,0:T(8,128)(2,1)S(1)}, bf16[128,512]{1,0:T(8,128)(2,1)S(1)}, u32[]{:S(2)}, u32[]{:S(2)}) collective-permute-start(bf16[128,512]{1,0:T(8,128)(2,1)S(1)} %collective-permute-done.2), channel_id=1, source_target_pairs={{0,2},{2,4},{4,6},{6,8},{8,10},{10,12},{12,14},{14,16},{16,18},{18... | collective-permute-start | bytes 393224 | tf_op jit(solution)/shard_map/ppermute | solution.py:33
  43.0 8.6 %collective-permute-start.4 = (bf16[128,512]{1,0:T(8,128)(2,1)S(1)}, bf16[128,512]{1,0:T(8,128)(2,1)S(1)}, u32[]{:S(2)}, u32[]{:S(2)}) collective-permute-start(bf16[128,512]{1,0:T(8,128)(2,1)S(1)} %collective-permute-done.3), channel_id=1, source_target_pairs={{0,2},{2,4},{4,6},{6,8},{8,10},{10,12},{12,14},{14,16},{16,18},{18... | collective-permute-start | bytes 393224 | tf_op jit(solution)/shard_map/ppermute | solution.py:33
  51.5 8.9 %collective-permute-start.5 = (bf16[128,512]{1,0:T(8,128)(2,1)S(1)}, bf16[128,512]{1,0:T(8,128)(2,1)S(1)}, u32[]{:S(2)}, u32[]{:S(2)}) collective-permute-start(bf16[128,512]{1,0:T(8,128)(2,1)S(1)} %collective-permute-done.4), channel_id=1, source_target_pairs={{0,2},{2,4},{4,6},{6,8},{8,10},{10,12},{12,14},{14,16},{16,18},{18... | collective-permute-start | bytes 393224 | tf_op jit(solution)/shard_map/ppermute | solution.py:33
  60.4 9.9 %collective-permute-start.6 = (bf16[128,512]{1,0:T(8,128)(2,1)S(1)}, bf16[128,512]{1,0:T(8,128)(2,1)S(1)}, u32[]{:S(2)}, u32[]{:S(2)}) collective-permute-start(bf16[128,512]{1,0:T(8,128)(2,1)S(1)} %collective-permute-done.5), channel_id=1, source_target_pairs={{0,2},{2,4},{4,6},{6,8},{8,10},{10,12},{12,14},{14,16},{16,18},{18... | collective-permute-start | bytes 393224 | tf_op jit(solution)/shard_map/ppermute | solution.py:33
  70.3 9.1 %collective-permute-start.7 = (bf16[128,512]{1,0:T(8,128)(2,1)S(1)}, bf16[128,512]{1,0:T(8,128)(2,1)S(1)}, u32[]{:S(2)}, u32[]{:S(2)}) collective-permute-start(bf16[128,512]{1,0:T(8,128)(2,1)S(1)} %collective-permute-done.6), channel_id=1, source_target_pairs={{0,2},{2,4},{4,6},{6,8},{8,10},{10,12},{12,14},{14,16},{16,18},{18... | collective-permute-start | bytes 393224 | tf_op jit(solution)/shard_map/ppermute | solution.py:33
  79.4 8.6 %collective-permute-start.8 = (bf16[128,512]{1,0:T(8,128)(2,1)S(1)}, bf16[128,512]{1,0:T(8,128)(2,1)S(1)}, u32[]{:S(2)}, u32[]{:S(2)}) collective-permute-start(bf16[128,512]{1,0:T(8,128)(2,1)S(1)} %collective-permute-done.7), channel_id=1, source_target_pairs={{0,2},{2,4},{4,6},{6,8},{8,10},{10,12},{12,14},{14,16},{16,18},{18... | collective-permute-start | bytes 393224 | tf_op jit(solution)/shard_map/ppermute | solution.py:33
  88.0 8.6 %collective-permute-start.9 = (bf16[128,512]{1,0:T(8,128)(2,1)S(1)}, bf16[128,512]{1,0:T(8,128)(2,1)S(1)}, u32[]{:S(2)}, u32[]{:S(2)}) collective-permute-start(bf16[128,512]{1,0:T(8,128)(2,1)S(1)} %collective-permute-done.8), channel_id=1, source_target_pairs={{0,2},{2,4},{4,6},{6,8},{8,10},{10,12},{12,14},{14,16},{16,18},{18... | collective-permute-start | bytes 393224 | tf_op jit(solution)/shard_map/ppermute | solution.py:33
  96.5 8.6 %collective-permute-start.10 = (bf16[128,512]{1,0:T(8,128)(2,1)S(1)}, bf16[128,512]{1,0:T(8,128)(2,1)S(1)}, u32[]{:S(2)}, u32[]{:S(2)}) collective-permute-start(bf16[128,512]{1,0:T(8,128)(2,1)S(1)} %collective-permute-done.9), channel_id=1, source_target_pairs={{0,2},{2,4},{4,6},{6,8},{8,10},{10,12},{12,14},{14,16},{16,18},{18... | collective-permute-start | bytes 393224 | tf_op jit(solution)/shard_map/ppermute | solution.py:33
  105.1 8.6 %collective-permute-start.11 = (bf16[128,512]{1,0:T(8,128)(2,1)S(1)}, bf16[128,512]{1,0:T(8,128)(2,1)S(1)}, u32[]{:S(2)}, u32[]{:S(2)}) collective-permute-start(bf16[128,512]{1,0:T(8,128)(2,1)S(1)} %collective-permute-done.10), channel_id=1, source_target_pairs={{0,2},{2,4},{4,6},{6,8},{8,10},{10,12},{12,14},{14,16},{16,18},{18... | collective-permute-start | bytes 393224 | tf_op jit(solution)/shard_map/ppermute | solution.py:33
  113.6 8.9 %collective-permute-start.12 = (bf16[128,512]{1,0:T(8,128)(2,1)S(1)}, bf16[128,512]{1,0:T(8,128)(2,1)S(1)}, u32[]{:S(2)}, u32[]{:S(2)}) collective-permute-start(bf16[128,512]{1,0:T(8,128)(2,1)S(1)} %collective-permute-done.11), channel_id=1, source_target_pairs={{0,2},{2,4},{4,6},{6,8},{8,10},{10,12},{12,14},{14,16},{16,18},{18... | collective-permute-start | bytes 393224 | tf_op jit(solution)/shard_map/ppermute | solution.py:33
  113.7 119.3 %reduce-scatter.2.cloned.1.call-start = ((), (), s32[]{:S(2)}) async-start(), calls=%async_computation.2 | async-start | bytes 1572864 | tf_op jit(solution)/shard_map/reduce_scatter | solution.py:78
  122.5 9.6 %collective-permute-start.13 = (bf16[128,512]{1,0:T(8,128)(2,1)S(1)}, bf16[128,512]{1,0:T(8,128)(2,1)S(1)}, u32[]{:S(2)}, u32[]{:S(2)}) collective-permute-start(bf16[128,512]{1,0:T(8,128)(2,1)S(1)} %collective-permute-done.12), channel_id=1, source_target_pairs={{0,2},{2,4},{4,6},{6,8},{8,10},{10,12},{12,14},{14,16},{16,18},{18... | collective-permute-start | bytes 393224 | tf_op jit(solution)/shard_map/ppermute | solution.py:33
  132.2 8.6 %collective-permute-start.14 = (bf16[128,512]{1,0:T(8,128)(2,1)S(1)}, bf16[128,512]{1,0:T(8,128)(2,1)S(1)}, u32[]{:S(2)}, u32[]{:S(2)}) collective-permute-start(bf16[128,512]{1,0:T(8,128)(2,1)S(1)} %collective-permute-done.13), channel_id=1, source_target_pairs={{0,2},{2,4},{4,6},{6,8},{8,10},{10,12},{12,14},{14,16},{16,18},{18... | collective-permute-start | bytes 393224 | tf_op jit(solution)/shard_map/ppermute | solution.py:33
  180.6 2.2 copy-start.1
  187.4 5.8 %copy-start = (f32[4,1024,128,4]{2,1,3,0:T(8,128)S(1)}, f32[4,1024,128,4]{2,1,3,0:T(8,128)}, u32[]{:S(2)}) copy-start(f32[4,1024,128,4]{2,1,3,0:T(8,128)} %get-tuple-element.184) | copy-start | bytes 25165828 | tf_op jit(solution)/shard_map/while
  197.2 2.2 copy-start.1
  204.0 5.8 %copy-start = (f32[4,1024,128,4]{2,1,3,0:T(8,128)S(1)}, f32[4,1024,128,4]{2,1,3,0:T(8,128)}, u32[]{:S(2)}) copy-start(f32[4,1024,128,4]{2,1,3,0:T(8,128)} %get-tuple-element.184) | copy-start | bytes 25165828 | tf_op jit(solution)/shard_map/while
  216.3 9.2 %copy-start.4 = (bf16[2048]{0:T(1024)(128)(2,1)S(1)}, bf16[2048]{0:T(1024)(128)(2,1)}, u32[]{:S(2)}) copy-start(bf16[2048]{0:T(1024)(128)(2,1)} %param.14) | copy-start | bytes 12292
  216.3 16.6 %copy-start.2 = (bf16[128,2048]{1,0:T(8,128)(2,1)S(1)}, bf16[128,2048]{1,0:T(8,128)(2,1)}, u32[]{:S(2)}) copy-start(bf16[128,2048]{1,0:T(8,128)(2,1)} %param.13) | copy-start | bytes 1572868
Sparse Core Ops, SparseCore 0:
  113.8 62.5 all-gather.1
  225.7 7.1 reduce-scatter.1
